TPU v7x, 256 devices: a whole 4x4x8 slice. The times are simulated.
256 devices in a mesh: sec: 4 (over y_lo, core), mom: 8 (over x, y_hi), en: 8 (over z).
Axes of the slice: x: 4, y: 4 (y_hi: 2, y_lo: 2; y = y_hi * 2 + y_lo), z: 8, core: 2. Of those that a mesh axis runs over, the one named last changes fastest.
Arguments:
- green_blocks: bfloat16 [8, 64, 2, 128, 128], P('mom', ('sec', 'en')), may hold values from -6 to 6
- derivative: bfloat16 [3, 128, 128], replicated, may hold values from -0.5 to 0.5
- bare_phonon: float32 [4, 8, 2, 3, 3, 128], P('sec', 'mom'), may hold values from -4 to 4
- prior_polar: float32 [4, 8, 2, 3, 3, 128], P('sec', 'mom'), may hold values from -4 to 4
- offsets: int32 [4], replicated, may hold values from 1 to 2, as said below
- momenta: int32 [8, 8], replicated, may hold values from 0 to 7, as said below
Outputs:
- sigma: float32 [8, 64, 2, 128, 128], P('mom', ('sec', 'en'))
- polarization: float32 [4, 8, 3, 128], P('sec', 'mom')
Inputs may be any that keep to these rules, and one draw needn't show every extreme that they name: `offsets`: every mode's offset lies in 1 to 2; some mode's offset equals 2 and another mode's equals 1. momenta[k, k'] = p((k - k') mod 8) for a permutation p of the 8 phonon momenta.
All inputs are finite; a program needn't handle non-finite values.
Results may differ from a plain program's by a relative error of at most 0.014.
Values may be sent and summed in bfloat16 or wider, within the bound.
No kernel may reach another device: no remote copies, remote signals or barrier semaphores. Data moves between devices by JAX's collectives and lax.ppermute only.
A program may use at most 64 MiB of HBM per device.

v0:
```python
import math
import jax
import jax.numpy as jnp
from jax import lax
from jax.sharding import PartitionSpec as P


def passed_along(x, axis, by):
    peers = lax.axis_size(axis)
    pairs = [(i, i + by) for i in range(peers) if 0 <= i + by < peers]
    return lax.ppermute(x, axis, pairs)


def contract(former, latter):
    return jnp.sum(former[..., :, :, None, :] * latter[..., None, :, :, :], axis=-3)


def complex_product(former, latter):
    real_part = contract(former[..., 0, :, :, :], latter[..., 0, :, :, :]) - contract(
        former[..., 1, :, :, :], latter[..., 1, :, :, :]
    )
    imag_part = contract(former[..., 0, :, :, :], latter[..., 1, :, :, :]) + contract(
        former[..., 1, :, :, :], latter[..., 0, :, :, :]
    )
    return jnp.stack([real_part, imag_part], axis=-4)


def dyson_update(bare_phonon, prior_polar):
    return bare_phonon + complex_product(complex_product(bare_phonon, prior_polar), bare_phonon)


def flipped_products(blocks, derivative):
    flipped = jnp.einsum(
        "ktcbx,ixa->kticab", blocks, derivative, preferred_element_type=jnp.float32
    )
    sign_flip = jnp.array([1.0, -1.0], jnp.float32).reshape(1, 1, 1, 2, 1, 1)
    return (flipped * sign_flip).astype(jnp.bfloat16)


def mode_weights(chosen):
    real_part = chosen[:, :, 0]
    imag_part = chosen[:, :, 1]
    upper_part = jnp.stack([real_part, -imag_part], axis=2)
    lower_part = jnp.stack([imag_part, real_part], axis=2)
    return jnp.stack([upper_part, lower_part], axis=2)


def weighted_rows(weights, selected):
    mode_count = weights.shape[1]
    total = None
    for mode_index in range(mode_count):
        for part_index in range(2):
            for direction in range(3):
                factor = jnp.transpose(
                    weights[:, mode_index, :, part_index, direction, :, :], (0, 2, 1, 3)
                )
                slab = selected[direction, :, mode_index, part_index].astype(jnp.float32)
                term = factor[:, None, :, :, :, None] * slab[None, :, None, None, :, :]
                total = term if total is None else total + term
    return total.astype(jnp.bfloat16)


def point_terms(source, chosen, derivative, offsets, targets, levels, flipped):
    blocks = jnp.einsum(
        "iab,scbd->iscad", derivative, source, preferred_element_type=jnp.float32
    ).astype(jnp.bfloat16)
    mode_count = chosen.shape[1]
    selected = jnp.stack(
        [
            lax.dynamic_slice_in_dim(blocks, levels - offsets[mode_index], targets, 1)
            for mode_index in range(mode_count)
        ],
        axis=2,
    )
    weights = mode_weights(chosen)
    combined = weighted_rows(weights, selected)
    sigma_part = jnp.einsum(
        "ktjxab,jbd->ktxad", combined, derivative, preferred_element_type=jnp.float32
    )
    polar_part = jnp.einsum(
        "itmcab,kticab->kmia", selected, flipped, preferred_element_type=jnp.float32
    )
    return (sigma_part, polar_part)


def per_device(green_blocks, derivative, bare_phonon, prior_polar, offsets, momenta):
    points = green_blocks.shape[0]
    levels = green_blocks.shape[1]
    block_order = green_blocks.shape[-1]
    all_points = points * lax.axis_size("mom")
    all_levels = levels * lax.axis_size("sec") * lax.axis_size("en")
    phonon = dyson_update(bare_phonon, prior_polar)
    local_modes = phonon.shape[0]
    stacked = phonon.reshape((local_modes * points,) + phonon.shape[2:])
    gathered = lax.all_gather(stacked, ("sec", "mom"), axis=0, tiled=True)
    mode_count = gathered.shape[0] // all_points
    phonon_table = jnp.transpose(
        gathered.reshape((mode_count, all_points) + phonon.shape[2:]), (1, 0, 2, 3, 4, 5)
    )
    own_rows = lax.dynamic_slice_in_dim(momenta, lax.axis_index("mom") * points, points, 0)
    momentum_ids = lax.broadcasted_iota(jnp.int32, (points, all_points), 1)
    lower_rim = passed_along(green_blocks, ("sec", "en"), 1)
    travelling = jnp.concatenate([lower_rim, green_blocks], axis=1)
    targets = green_blocks.shape[1]
    flipped = flipped_products(green_blocks, derivative)
    initial = (
        jnp.zeros((points, targets, 2, block_order, block_order), jnp.float32),
        jnp.zeros((all_points, mode_count, 3, block_order), jnp.float32),
    )
    pieces = lax.all_gather(travelling, "mom", axis=0, tiled=True)

    def one_point(position, running):
        sigma_sum, polar_sum = running
        source = lax.dynamic_index_in_dim(pieces, position, 0, keepdims=False)
        column = lax.dynamic_index_in_dim(own_rows, position, 1, keepdims=False)
        onehot = (column[:, None] == momentum_ids).astype(jnp.float32)
        chosen = jnp.einsum(
            "kq,qmxija->kmxija", onehot, phonon_table, precision=lax.Precision.HIGHEST
        )
        sigma_part, polar_part = point_terms(
            source, chosen, derivative, offsets, targets, levels, flipped
        )
        polar_sum = polar_sum + jnp.einsum(
            "kq,kmia->qmia", onehot, polar_part, precision=lax.Precision.HIGHEST
        )
        return (sigma_sum + sigma_part, polar_sum)

    sigma_sum, polar_sum = lax.fori_loop(0, pieces.shape[0], one_point, initial)
    sigma_scale = 1.0 / math.sqrt(9.0 * mode_count * all_points)
    polar_scale = 1.0 / math.sqrt(float(all_points * all_levels * block_order))
    ordered = jnp.transpose(polar_sum, (1, 0, 2, 3))
    summed = lax.psum(ordered, ("sec", "mom", "en"))
    own_share = lax.dynamic_slice(
        summed,
        (lax.axis_index("sec") * local_modes, lax.axis_index("mom") * points, 0, 0),
        (local_modes, points, 3, block_order),
    )
    return (sigma_sum * sigma_scale, own_share * polar_scale)


def solution(mesh):
    return jax.shard_map(
        per_device,
        mesh=mesh,
        in_specs=(
            P("mom", ("sec", "en"), None, None, None),
            P(),
            P("sec", "mom", None, None, None, None),
            P("sec", "mom", None, None, None, None),
            P(),
            P(),
        ),
        out_specs=(P("mom", ("sec", "en"), None, None, None), P("sec", "mom", None, None)),
        check_vma=False,
    )
```

profile of v0, /device:TPU:1, one launch (start us, length us, event | category | flops | bytes accessed | tf_op | source)
XLA Modules:
  0.0 422.1 jit_solution(5566107944990981499)
XLA Ops:
  7.3 4.5 %collective-permute-start = (bf16[1,2,2,128,128]{4,3,2,1,0:T(8,128)(2,1)}, bf16[1,2,2,128,128]{4,3,2,1,0:T(8,128)(2,1)S(1)}, u32[]{:S(2)}, u32[]{:S(2)}) collective-permute-start(bf16[1,2,2,128,128]{4,3,2,1,0:T(8,128)(2,1)} %param.9), channel_id=1, source_target_pairs={{0,1},{1,2},{2,3},{3,4},{4,5},{5,6},{6,7},{7,64},{64,65},{65,66},{... | collective-permute-start | bytes 393224 | tf_op jit(solution)/shard_map/ppermute | solution.py:11
  11.8 7.9 %collective-permute-done = bf16[1,2,2,128,128]{4,3,2,1,0:T(8,128)(2,1)S(1)} collective-permute-done((bf16[1,2,2,128,128]{4,3,2,1,0:T(8,128)(2,1)}, bf16[1,2,2,128,128]{4,3,2,1,0:T(8,128)(2,1)S(1)}, u32[]{:S(2)}, u32[]{:S(2)}) %collective-permute-start) | collective-permute-done | bytes 131104 | tf_op jit(solution)/shard_map/ppermute | solution.py:11
  19.7 1.6 pad_maximum_fusion.1
  21.3 1.5 fusion.141
  30.5 69.0 %all-gather = f32[32,1,2,3,3,128]{5,2,4,3,1,0:T(2,128)S(1)} all-gather(f32[1,1,2,3,3,128]{5,2,4,3,1,0:T(2,128)S(1)} %copy.131), channel_id=2, replica_groups=mesh['sec'=4,'mom'=8,'en'=8] {'sec','mom'}, dimensions={0}, use_global_device_ids=true | all-gather | bytes 304128 | tf_op jit(solution)/shard_map/all_gather | solution.py:95
  100.7 235.9 %while.19 = (s32[]{:T(128)}, f32[1,2,2,128,128]{4,3,2,1,0:T(8,128)}, f32[8,4,3,128]{3,2,1,0:T(4,128)}, s32[1,8]{1,0:T(1,128)}, f32[8,4,2,3,3,128]{5,4,3,2,1,0:T(...) while((s32[]{:T(128)}, ...), condition=%wide.region_9.10_spmd.clone, body=%wide.region_8.9_spmd.clone.sunk | while | flops 167619600 | bytes 31974176 | solution.py:128
  100.7 1.3 constant_dynamic-slice_fusion.3
  102.0 1.3 bitcast_convert_fusion.5
  103.3 1.1 fusion.161
  105.8 1.4 convolution_convert_fusion.2
  123.1 6.8 %fusion.167 = f32[1,2,2,128,128]{4,3,2,1,0:T(8,128)} fusion(f32[2,128,128]{2,1,0:T(8,128)S(1)} %copy-done.12, f32[3,2,128]{2,0,1:T(4,128)S(1)} %get-tuple-element.669, f32[2,128,128]{2,1,0:T(8,128)S(1)} %copy-done.13, f32[3,2,128]{2,0,1:T(4,128)S(1)} %get-tuple-element.671, f32[2,128,128]{2,1,0:T(8,128)} %copy.209, ...), kind=kOutput, calls=%fused_computation.5.clone.1 | convolution fusion | flops 59899904 | bytes 3842049 | tf_op jit(solution)/shard_map/while/body/eval_jaxpr/ktjxab,jbd->ktxad/dot_general | solution.py:77
  129.9 1.3 constant_dynamic-slice_fusion.3
  131.3 1.3 bitcast_convert_fusion.5
  132.5 1.1 fusion.161
  135.0 1.4 convolution_convert_fusion.2
  152.4 7.1 %fusion.167 = f32[1,2,2,128,128]{4,3,2,1,0:T(8,128)} fusion(f32[2,128,128]{2,1,0:T(8,128)S(1)} %copy-done.12, f32[3,2,128]{2,0,1:T(4,128)S(1)} %get-tuple-element.669, f32[2,128,128]{2,1,0:T(8,128)S(1)} %copy-done.13, f32[3,2,128]{2,0,1:T(4,128)S(1)} %get-tuple-element.671, f32[2,128,128]{2,1,0:T(8,128)} %copy.209, ...), kind=kOutput, calls=%fused_computation.5.clone.1 | convolution fusion | flops 59899904 | bytes 3842049 | tf_op jit(solution)/shard_map/while/body/eval_jaxpr/ktjxab,jbd->ktxad/dot_general | solution.py:77
  159.4 1.3 constant_dynamic-slice_fusion.3
  160.8 1.3 bitcast_convert_fusion.5
  162.1 1.1 fusion.161
  164.5 1.4 convolution_convert_fusion.2
  181.9 7.1 %fusion.167 = f32[1,2,2,128,128]{4,3,2,1,0:T(8,128)} fusion(f32[2,128,128]{2,1,0:T(8,128)S(1)} %copy-done.12, f32[3,2,128]{2,0,1:T(4,128)S(1)} %get-tuple-element.669, f32[2,128,128]{2,1,0:T(8,128)S(1)} %copy-done.13, f32[3,2,128]{2,0,1:T(4,128)S(1)} %get-tuple-element.671, f32[2,128,128]{2,1,0:T(8,128)} %copy.209, ...), kind=kOutput, calls=%fused_computation.5.clone.1 | convolution fusion | flops 59899904 | bytes 3842049 | tf_op jit(solution)/shard_map/while/body/eval_jaxpr/ktjxab,jbd->ktxad/dot_general | solution.py:77
  189.0 1.3 constant_dynamic-slice_fusion.3
  190.3 1.3 bitcast_convert_fusion.5
  191.6 1.1 fusion.161
  194.1 1.3 convolution_convert_fusion.2
  211.4 7.1 %fusion.167 = f32[1,2,2,128,128]{4,3,2,1,0:T(8,128)} fusion(f32[2,128,128]{2,1,0:T(8,128)S(1)} %copy-done.12, f32[3,2,128]{2,0,1:T(4,128)S(1)} %get-tuple-element.669, f32[2,128,128]{2,1,0:T(8,128)S(1)} %copy-done.13, f32[3,2,128]{2,0,1:T(4,128)S(1)} %get-tuple-element.671, f32[2,128,128]{2,1,0:T(8,128)} %copy.209, ...), kind=kOutput, calls=%fused_computation.5.clone.1 | convolution fusion | flops 59899904 | bytes 3842049 | tf_op jit(solution)/shard_map/while/body/eval_jaxpr/ktjxab,jbd->ktxad/dot_general | solution.py:77
  218.5 1.3 constant_dynamic-slice_fusion.3
  219.8 1.3 bitcast_convert_fusion.5
  221.1 1.1 fusion.161
  223.6 1.4 convolution_convert_fusion.2
  240.9 7.1 %fusion.167 = f32[1,2,2,128,128]{4,3,2,1,0:T(8,128)} fusion(f32[2,128,128]{2,1,0:T(8,128)S(1)} %copy-done.12, f32[3,2,128]{2,0,1:T(4,128)S(1)} %get-tuple-element.669, f32[2,128,128]{2,1,0:T(8,128)S(1)} %copy-done.13, f32[3,2,128]{2,0,1:T(4,128)S(1)} %get-tuple-element.671, f32[2,128,128]{2,1,0:T(8,128)} %copy.209, ...), kind=kOutput, calls=%fused_computation.5.clone.1 | convolution fusion | flops 59899904 | bytes 3842049 | tf_op jit(solution)/shard_map/while/body/eval_jaxpr/ktjxab,jbd->ktxad/dot_general | solution.py:77
  248.0 1.3 constant_dynamic-slice_fusion.3
  249.3 1.3 bitcast_convert_fusion.5
  250.6 1.1 fusion.161
  253.1 1.4 convolution_convert_fusion.2
  270.5 7.1 %fusion.167 = f32[1,2,2,128,128]{4,3,2,1,0:T(8,128)} fusion(f32[2,128,128]{2,1,0:T(8,128)S(1)} %copy-done.12, f32[3,2,128]{2,0,1:T(4,128)S(1)} %get-tuple-element.669, f32[2,128,128]{2,1,0:T(8,128)S(1)} %copy-done.13, f32[3,2,128]{2,0,1:T(4,128)S(1)} %get-tuple-element.671, f32[2,128,128]{2,1,0:T(8,128)} %copy.209, ...), kind=kOutput, calls=%fused_computation.5.clone.1 | convolution fusion | flops 59899904 | bytes 3842049 | tf_op jit(solution)/shard_map/while/body/eval_jaxpr/ktjxab,jbd->ktxad/dot_general | solution.py:77
  277.5 1.3 constant_dynamic-slice_fusion.3
  278.9 1.3 bitcast_convert_fusion.5
  280.1 1.1 fusion.161
  282.6 1.4 convolution_convert_fusion.2
  300.0 7.1 %fusion.167 = f32[1,2,2,128,128]{4,3,2,1,0:T(8,128)} fusion(f32[2,128,128]{2,1,0:T(8,128)S(1)} %copy-done.12, f32[3,2,128]{2,0,1:T(4,128)S(1)} %get-tuple-element.669, f32[2,128,128]{2,1,0:T(8,128)S(1)} %copy-done.13, f32[3,2,128]{2,0,1:T(4,128)S(1)} %get-tuple-element.671, f32[2,128,128]{2,1,0:T(8,128)} %copy.209, ...), kind=kOutput, calls=%fused_computation.5.clone.1 | convolution fusion | flops 59899904 | bytes 3842049 | tf_op jit(solution)/shard_map/while/body/eval_jaxpr/ktjxab,jbd->ktxad/dot_general | solution.py:77
  307.1 1.3 constant_dynamic-slice_fusion.3
  308.4 1.3 bitcast_convert_fusion.5
  309.7 1.1 fusion.161
  312.1 1.4 convolution_convert_fusion.2
  329.5 7.1 %fusion.167 = f32[1,2,2,128,128]{4,3,2,1,0:T(8,128)} fusion(f32[2,128,128]{2,1,0:T(8,128)S(1)} %copy-done.12, f32[3,2,128]{2,0,1:T(4,128)S(1)} %get-tuple-element.669, f32[2,128,128]{2,1,0:T(8,128)S(1)} %copy-done.13, f32[3,2,128]{2,0,1:T(4,128)S(1)} %get-tuple-element.671, f32[2,128,128]{2,1,0:T(8,128)} %copy.209, ...), kind=kOutput, calls=%fused_computation.5.clone.1 | convolution fusion | flops 59899904 | bytes 3842049 | tf_op jit(solution)/shard_map/while/body/eval_jaxpr/ktjxab,jbd->ktxad/dot_general | solution.py:77
  337.4 75.5 %psum.7 = f32[4,8,3,128]{3,1,2,0:T(8,128)S(1)} all-reduce(f32[4,8,3,128]{3,1,2,0:T(8,128)S(1)} %bitcast.412), channel_id=1, replica_groups=mesh['sec'=4,'mom'=8,'en'=8] {'sec','mom','en'}, use_global_device_ids=true, to_apply=%region_10.11 | all-reduce | flops 12288 | bytes 98304 | tf_op jit(solution)/shard_map/psum | solution.py:132
  413.0 1.7 broadcast_multiply_fusion
  (576 shorter events, 141.5 us)
Async XLA Ops:
  7.2 92.9 %copy-start = (s32[8,8]{1,0:T(8,128)S(1)}, s32[8,8]{1,0:T(8,128)}, u32[]{:S(2)}) copy-start(s32[8,8]{1,0:T(8,128)} %param.14) | copy-start | bytes 772
  7.2 92.5 %copy-start.18 = (f32[2]{0:T(128)S(1)}, f32[2]{0:T(128)}, u32[]{:S(2)}) copy-start(f32[2]{0:T(128)} %constant.97.clone) | copy-start | bytes 28
  7.2 92.5 %copy-start.16 = (bf16[1,2,2,128,128]{4,3,2,1,0:T(8,128)(2,1)S(1)}, bf16[1,2,2,128,128]{4,3,2,1,0:T(8,128)(2,1)}, u32[]{:S(2)}) copy-start(bf16[1,2,2,128,128]{4,3,2,1,0:T(8,128)(2,1)} %param.9) | copy-start | bytes 393220
  7.2 92.5 %copy-start.1 = (bf16[3,128,128]{2,1,0:T(8,128)(2,1)S(1)}, bf16[3,128,128]{2,1,0:T(8,128)(2,1)}, u32[]{:S(2)}) copy-start(bf16[3,128,128]{2,1,0:T(8,128)(2,1)} %param.10) | copy-start | bytes 294916
  7.2 93.5 %all-gather.3.cloned.1.call-start = ((), (), s32[]{:S(2)}) async-start(), calls=%async_computation | async-start | bytes 2359296 | tf_op jit(solution)/shard_map/all_gather | solution.py:110
  7.3 12.4 %collective-permute-start = (bf16[1,2,2,128,128]{4,3,2,1,0:T(8,128)(2,1)}, bf16[1,2,2,128,128]{4,3,2,1,0:T(8,128)(2,1)S(1)}, u32[]{:S(2)}, u32[]{:S(2)}) collective-permute-start(bf16[1,2,2,128,128]{4,3,2,1,0:T(8,128)(2,1)} %param.9), channel_id=1, source_target_pairs={{0,1},{1,2},{2,3},{3,4},{4,5},{5,6},{6,7},{7,64},{64,65},{65,66},{... | collective-permute-start | bytes 393224 | tf_op jit(solution)/shard_map/ppermute | solution.py:11
  117.1 5.9 %copy-start.2 = (f32[2,128,128]{2,1,0:T(8,128)S(1)}, f32[2,128,128]{2,1,0:T(8,128)}, u32[]{:S(2)}) copy-start(f32[2,128,128]{2,1,0:T(8,128)} %copy.221) | copy-start | bytes 393220 | tf_op jit(solution)/shard_map/while
  117.2 5.9 %copy-start.3 = (f32[2,128,128]{2,1,0:T(8,128)S(1)}, f32[2,128,128]{2,1,0:T(8,128)}, u32[]{:S(2)}) copy-start(f32[2,128,128]{2,1,0:T(8,128)} %copy.222) | copy-start | bytes 393220 | tf_op jit(solution)/shard_map/while
  117.2 5.9 %copy-start.4 = (f32[2,128,128]{2,1,0:T(8,128)S(1)}, f32[2,128,128]{2,1,0:T(8,128)}, u32[]{:S(2)}) copy-start(f32[2,128,128]{2,1,0:T(8,128)} %copy.223) | copy-start | bytes 393220 | tf_op jit(solution)/shard_map/while
  117.2 5.9 %copy-start.5 = (f32[2,128,128]{2,1,0:T(8,128)S(1)}, f32[2,128,128]{2,1,0:T(8,128)}, u32[]{:S(2)}) copy-start(f32[2,128,128]{2,1,0:T(8,128)} %copy.224) | copy-start | bytes 393220 | tf_op jit(solution)/shard_map/while
  117.2 5.9 %copy-start.6 = (f32[2,128,128]{2,1,0:T(8,128)S(1)}, f32[2,128,128]{2,1,0:T(8,128)}, u32[]{:S(2)}) copy-start(f32[2,128,128]{2,1,0:T(8,128)} %copy.225) | copy-start | bytes 393220 | tf_op jit(solution)/shard_map/while
  117.2 5.9 %copy-start.7 = (f32[2,128,128]{2,1,0:T(8,128)S(1)}, f32[2,128,128]{2,1,0:T(8,128)}, u32[]{:S(2)}) copy-start(f32[2,128,128]{2,1,0:T(8,128)} %copy.226) | copy-start | bytes 393220 | tf_op jit(solution)/shard_map/while
  146.4 5.9 %copy-start.2 = (f32[2,128,128]{2,1,0:T(8,128)S(1)}, f32[2,128,128]{2,1,0:T(8,128)}, u32[]{:S(2)}) copy-start(f32[2,128,128]{2,1,0:T(8,128)} %copy.221) | copy-start | bytes 393220 | tf_op jit(solution)/shard_map/while
  146.4 5.9 %copy-start.3 = (f32[2,128,128]{2,1,0:T(8,128)S(1)}, f32[2,128,128]{2,1,0:T(8,128)}, u32[]{:S(2)}) copy-start(f32[2,128,128]{2,1,0:T(8,128)} %copy.222) | copy-start | bytes 393220 | tf_op jit(solution)/shard_map/while
  146.4 5.9 %copy-start.4 = (f32[2,128,128]{2,1,0:T(8,128)S(1)}, f32[2,128,128]{2,1,0:T(8,128)}, u32[]{:S(2)}) copy-start(f32[2,128,128]{2,1,0:T(8,128)} %copy.223) | copy-start | bytes 393220 | tf_op jit(solution)/shard_map/while
  146.4 5.9 %copy-start.5 = (f32[2,128,128]{2,1,0:T(8,128)S(1)}, f32[2,128,128]{2,1,0:T(8,128)}, u32[]{:S(2)}) copy-start(f32[2,128,128]{2,1,0:T(8,128)} %copy.224) | copy-start | bytes 393220 | tf_op jit(solution)/shard_map/while
  146.4 5.9 %copy-start.6 = (f32[2,128,128]{2,1,0:T(8,128)S(1)}, f32[2,128,128]{2,1,0:T(8,128)}, u32[]{:S(2)}) copy-start(f32[2,128,128]{2,1,0:T(8,128)} %copy.225) | copy-start | bytes 393220 | tf_op jit(solution)/shard_map/while
  146.4 5.9 %copy-start.7 = (f32[2,128,128]{2,1,0:T(8,128)S(1)}, f32[2,128,128]{2,1,0:T(8,128)}, u32[]{:S(2)}) copy-start(f32[2,128,128]{2,1,0:T(8,128)} %copy.226) | copy-start | bytes 393220 | tf_op jit(solution)/shard_map/while
  175.9 5.9 %copy-start.2 = (f32[2,128,128]{2,1,0:T(8,128)S(1)}, f32[2,128,128]{2,1,0:T(8,128)}, u32[]{:S(2)}) copy-start(f32[2,128,128]{2,1,0:T(8,128)} %copy.221) | copy-start | bytes 393220 | tf_op jit(solution)/shard_map/while
  175.9 5.9 %copy-start.3 = (f32[2,128,128]{2,1,0:T(8,128)S(1)}, f32[2,128,128]{2,1,0:T(8,128)}, u32[]{:S(2)}) copy-start(f32[2,128,128]{2,1,0:T(8,128)} %copy.222) | copy-start | bytes 393220 | tf_op jit(solution)/shard_map/while
  175.9 5.9 %copy-start.4 = (f32[2,128,128]{2,1,0:T(8,128)S(1)}, f32[2,128,128]{2,1,0:T(8,128)}, u32[]{:S(2)}) copy-start(f32[2,128,128]{2,1,0:T(8,128)} %copy.223) | copy-start | bytes 393220 | tf_op jit(solution)/shard_map/while
  175.9 5.9 %copy-start.5 = (f32[2,128,128]{2,1,0:T(8,128)S(1)}, f32[2,128,128]{2,1,0:T(8,128)}, u32[]{:S(2)}) copy-start(f32[2,128,128]{2,1,0:T(8,128)} %copy.224) | copy-start | bytes 393220 | tf_op jit(solution)/shard_map/while
  175.9 5.9 %copy-start.6 = (f32[2,128,128]{2,1,0:T(8,128)S(1)}, f32[2,128,128]{2,1,0:T(8,128)}, u32[]{:S(2)}) copy-start(f32[2,128,128]{2,1,0:T(8,128)} %copy.225) | copy-start | bytes 393220 | tf_op jit(solution)/shard_map/while
  176.0 5.9 %copy-start.7 = (f32[2,128,128]{2,1,0:T(8,128)S(1)}, f32[2,128,128]{2,1,0:T(8,128)}, u32[]{:S(2)}) copy-start(f32[2,128,128]{2,1,0:T(8,128)} %copy.226) | copy-start | bytes 393220 | tf_op jit(solution)/shard_map/while
  205.4 5.9 %copy-start.2 = (f32[2,128,128]{2,1,0:T(8,128)S(1)}, f32[2,128,128]{2,1,0:T(8,128)}, u32[]{:S(2)}) copy-start(f32[2,128,128]{2,1,0:T(8,128)} %copy.221) | copy-start | bytes 393220 | tf_op jit(solution)/shard_map/while
  205.4 5.9 %copy-start.3 = (f32[2,128,128]{2,1,0:T(8,128)S(1)}, f32[2,128,128]{2,1,0:T(8,128)}, u32[]{:S(2)}) copy-start(f32[2,128,128]{2,1,0:T(8,128)} %copy.222) | copy-start | bytes 393220 | tf_op jit(solution)/shard_map/while
  205.4 5.9 %copy-start.4 = (f32[2,128,128]{2,1,0:T(8,128)S(1)}, f32[2,128,128]{2,1,0:T(8,128)}, u32[]{:S(2)}) copy-start(f32[2,128,128]{2,1,0:T(8,128)} %copy.223) | copy-start | bytes 393220 | tf_op jit(solution)/shard_map/while
  205.5 5.9 %copy-start.5 = (f32[2,128,128]{2,1,0:T(8,128)S(1)}, f32[2,128,128]{2,1,0:T(8,128)}, u32[]{:S(2)}) copy-start(f32[2,128,128]{2,1,0:T(8,128)} %copy.224) | copy-start | bytes 393220 | tf_op jit(solution)/shard_map/while
  205.5 5.9 %copy-start.6 = (f32[2,128,128]{2,1,0:T(8,128)S(1)}, f32[2,128,128]{2,1,0:T(8,128)}, u32[]{:S(2)}) copy-start(f32[2,128,128]{2,1,0:T(8,128)} %copy.225) | copy-start | bytes 393220 | tf_op jit(solution)/shard_map/while
  205.5 5.9 %copy-start.7 = (f32[2,128,128]{2,1,0:T(8,128)S(1)}, f32[2,128,128]{2,1,0:T(8,128)}, u32[]{:S(2)}) copy-start(f32[2,128,128]{2,1,0:T(8,128)} %copy.226) | copy-start | bytes 393220 | tf_op jit(solution)/shard_map/while
  234.9 5.9 %copy-start.2 = (f32[2,128,128]{2,1,0:T(8,128)S(1)}, f32[2,128,128]{2,1,0:T(8,128)}, u32[]{:S(2)}) copy-start(f32[2,128,128]{2,1,0:T(8,128)} %copy.221) | copy-start | bytes 393220 | tf_op jit(solution)/shard_map/while
  235.0 5.9 %copy-start.3 = (f32[2,128,128]{2,1,0:T(8,128)S(1)}, f32[2,128,128]{2,1,0:T(8,128)}, u32[]{:S(2)}) copy-start(f32[2,128,128]{2,1,0:T(8,128)} %copy.222) | copy-start | bytes 393220 | tf_op jit(solution)/shard_map/while
  235.0 5.9 %copy-start.4 = (f32[2,128,128]{2,1,0:T(8,128)S(1)}, f32[2,128,128]{2,1,0:T(8,128)}, u32[]{:S(2)}) copy-start(f32[2,128,128]{2,1,0:T(8,128)} %copy.223) | copy-start | bytes 393220 | tf_op jit(solution)/shard_map/while
  235.0 5.9 %copy-start.5 = (f32[2,128,128]{2,1,0:T(8,128)S(1)}, f32[2,128,128]{2,1,0:T(8,128)}, u32[]{:S(2)}) copy-start(f32[2,128,128]{2,1,0:T(8,128)} %copy.224) | copy-start | bytes 393220 | tf_op jit(solution)/shard_map/while
  235.0 5.9 %copy-start.6 = (f32[2,128,128]{2,1,0:T(8,128)S(1)}, f32[2,128,128]{2,1,0:T(8,128)}, u32[]{:S(2)}) copy-start(f32[2,128,128]{2,1,0:T(8,128)} %copy.225) | copy-start | bytes 393220 | tf_op jit(solution)/shard_map/while
  235.0 5.9 %copy-start.7 = (f32[2,128,128]{2,1,0:T(8,128)S(1)}, f32[2,128,128]{2,1,0:T(8,128)}, u32[]{:S(2)}) copy-start(f32[2,128,128]{2,1,0:T(8,128)} %copy.226) | copy-start | bytes 393220 | tf_op jit(solution)/shard_map/while
  264.5 5.9 %copy-start.2 = (f32[2,128,128]{2,1,0:T(8,128)S(1)}, f32[2,128,128]{2,1,0:T(8,128)}, u32[]{:S(2)}) copy-start(f32[2,128,128]{2,1,0:T(8,128)} %copy.221) | copy-start | bytes 393220 | tf_op jit(solution)/shard_map/while
  264.5 5.9 %copy-start.3 = (f32[2,128,128]{2,1,0:T(8,128)S(1)}, f32[2,128,128]{2,1,0:T(8,128)}, u32[]{:S(2)}) copy-start(f32[2,128,128]{2,1,0:T(8,128)} %copy.222) | copy-start | bytes 393220 | tf_op jit(solution)/shard_map/while
  264.5 5.9 %copy-start.4 = (f32[2,128,128]{2,1,0:T(8,128)S(1)}, f32[2,128,128]{2,1,0:T(8,128)}, u32[]{:S(2)}) copy-start(f32[2,128,128]{2,1,0:T(8,128)} %copy.223) | copy-start | bytes 393220 | tf_op jit(solution)/shard_map/while
  264.5 5.9 %copy-start.5 = (f32[2,128,128]{2,1,0:T(8,128)S(1)}, f32[2,128,128]{2,1,0:T(8,128)}, u32[]{:S(2)}) copy-start(f32[2,128,128]{2,1,0:T(8,128)} %copy.224) | copy-start | bytes 393220 | tf_op jit(solution)/shard_map/while
  264.5 5.9 %copy-start.6 = (f32[2,128,128]{2,1,0:T(8,128)S(1)}, f32[2,128,128]{2,1,0:T(8,128)}, u32[]{:S(2)}) copy-start(f32[2,128,128]{2,1,0:T(8,128)} %copy.225) | copy-start | bytes 393220 | tf_op jit(solution)/shard_map/while
  264.5 5.9 %copy-start.7 = (f32[2,128,128]{2,1,0:T(8,128)S(1)}, f32[2,128,128]{2,1,0:T(8,128)}, u32[]{:S(2)}) copy-start(f32[2,128,128]{2,1,0:T(8,128)} %copy.226) | copy-start | bytes 393220 | tf_op jit(solution)/shard_map/while
  294.0 5.9 %copy-start.2 = (f32[2,128,128]{2,1,0:T(8,128)S(1)}, f32[2,128,128]{2,1,0:T(8,128)}, u32[]{:S(2)}) copy-start(f32[2,128,128]{2,1,0:T(8,128)} %copy.221) | copy-start | bytes 393220 | tf_op jit(solution)/shard_map/while
  294.0 5.9 %copy-start.3 = (f32[2,128,128]{2,1,0:T(8,128)S(1)}, f32[2,128,128]{2,1,0:T(8,128)}, u32[]{:S(2)}) copy-start(f32[2,128,128]{2,1,0:T(8,128)} %copy.222) | copy-start | bytes 393220 | tf_op jit(solution)/shard_map/while
  294.0 5.9 %copy-start.4 = (f32[2,128,128]{2,1,0:T(8,128)S(1)}, f32[2,128,128]{2,1,0:T(8,128)}, u32[]{:S(2)}) copy-start(f32[2,128,128]{2,1,0:T(8,128)} %copy.223) | copy-start | bytes 393220 | tf_op jit(solution)/shard_map/while
  294.0 5.9 %copy-start.5 = (f32[2,128,128]{2,1,0:T(8,128)S(1)}, f32[2,128,128]{2,1,0:T(8,128)}, u32[]{:S(2)}) copy-start(f32[2,128,128]{2,1,0:T(8,128)} %copy.224) | copy-start | bytes 393220 | tf_op jit(solution)/shard_map/while
  294.0 5.9 %copy-start.6 = (f32[2,128,128]{2,1,0:T(8,128)S(1)}, f32[2,128,128]{2,1,0:T(8,128)}, u32[]{:S(2)}) copy-start(f32[2,128,128]{2,1,0:T(8,128)} %copy.225) | copy-start | bytes 393220 | tf_op jit(solution)/shard_map/while
  294.0 5.9 %copy-start.7 = (f32[2,128,128]{2,1,0:T(8,128)S(1)}, f32[2,128,128]{2,1,0:T(8,128)}, u32[]{:S(2)}) copy-start(f32[2,128,128]{2,1,0:T(8,128)} %copy.226) | copy-start | bytes 393220 | tf_op jit(solution)/shard_map/while
  (78 other events, 209.6 us)
Sparse Core Ops, SparseCore 0:
  21.4 60.3 all-gather.2
where the time goes:
time: 428 us; the launch traced here: 422 us
  blocking collectives  145 us (34%)
  local copies, waits for them, and re-layouts  135 us (32%)
  matrix products  76.3 us (18%)
  other arithmetic  31.9 us (7%)
  between operations  19.4 us (5%)
  waiting for transfers between devices  7.91 us (2%)
  starting transfers between devices  4.53 us (1%)
    mul x192, local copies, waits for them, and re-layouts, weighted_rows(): term = factor[:, None, :, :, :, None] * slab[None, :, None, None, :, :]  108 us
    psum x1, blocking collectives, per_device(): summed = lax.psum(ordered, ('sec', 'mom', 'en'))  75.5 us
    all_gather x1, blocking collectives, per_device(): gathered = lax.all_gather(stacked, ('sec', 'mom'), axis=0, tiled=True)  69 us
    dot_general x8, matrix products, point_terms(): jnp.einsum('ktjxab,jbd->ktxad', combined, derivative, preferred_element_t...  56.2 us
    mul x40, other arithmetic, weighted_rows(): term = factor[:, None, :, :, :, None] * slab[None, :, None, None, :, :]  12.7 us
    dot_general x8, matrix products, point_terms(): jnp.einsum('iab,scbd->iscad', derivative, source, preferred_element_type=...  10.8 us
    dynamic_slice x8, local copies, waits for them, and re-layouts, one_point(): column = lax.dynamic_index_in_dim(own_rows, position, 1, keepdims=False)  10.7 us
    another operation x8, other arithmetic  10.2 us
  transfers between devices with their start and end apart: 2, of which 1 were waited for; matrix products, arithmetic and copies ran while one was open for 1% of the time, Pallas kernels for 0%

commit v1 on v0

--- a/solution.py
+++ b/solution.py
@@ -129,7 +129,7 @@
     sigma_scale = 1.0 / math.sqrt(9.0 * mode_count * all_points)
     polar_scale = 1.0 / math.sqrt(float(all_points * all_levels * block_order))
     ordered = jnp.transpose(polar_sum, (1, 0, 2, 3))
-    summed = lax.psum(ordered, ("sec", "mom", "en"))
+    summed = jnp.sum(lax.all_gather(ordered, ("sec", "mom", "en")), axis=0)
     own_share = lax.dynamic_slice(
         summed,
         (lax.axis_index("sec") * local_modes, lax.axis_index("mom") * points, 0, 0),

time: 428 us -> 1090 us (2.55)
  waiting for transfers between devices: 7.91 us -> 736 us
  blocking collectives: 145 us -> 68.7 us
    all_gather x0 -> x1, waiting for transfers between devices: none -> 728 us  [per_device(): summed = jnp.sum(lax.all_gather(ordered, ('sec', 'mom', 'en')), axis=0)]
    psum x1 -> x0, blocking collectives: 75.5 us -> none  [per_device(): summed = lax.psum(ordered, ('sec', 'mom', 'en'))]
  transfers between devices with their start and end apart: 2 -> 3, of which waited for: 1 -> 2; matrix products, arithmetic and copies ran while one was open for 1% -> 1% of each run, Pallas kernels for 0% -> 0%
where the time goes in v1:
time: 1090 us; the launch traced here: 1080 us
  waiting for transfers between devices  736 us (68%)
  local copies, waits for them, and re-layouts  133 us (12%)
  matrix products  75.5 us (7%)
  blocking collectives  68.7 us (6%)
  other arithmetic  39.2 us (4%)
  between operations  19.4 us (2%)
    all_gather x1, waiting for transfers between devices, per_device(): summed = jnp.sum(lax.all_gather(ordered, ('sec', 'mom', 'en')), axis=0)  728 us
    mul x192, local copies, waits for them, and re-layouts, weighted_rows(): term = factor[:, None, :, :, :, None] * slab[None, :, None, None, :, :]  107 us
    all_gather x1, blocking collectives, per_device(): gathered = lax.all_gather(stacked, ('sec', 'mom'), axis=0, tiled=True)  68.7 us
    dot_general x8, matrix products, point_terms(): jnp.einsum('ktjxab,jbd->ktxad', combined, derivative, preferred_element_t...  56.2 us
  transfers between devices with their start and end apart: 3, of which 2 were waited for; matrix products, arithmetic and copies ran while one was open for 1% of the time, Pallas kernels for 0%

profile of v1, /device:TPU:1, one launch (start us, length us, event | category | flops | bytes accessed | tf_op | source)
XLA Modules:
  0.0 1079.2 jit_solution(4417534991939315481)
XLA Ops:
  7.3 4.5 collective-permute-start
  11.8 7.9 collective-permute-done
  19.7 1.6 pad_maximum_fusion.1
  21.4 1.5 fusion.141
  30.5 68.7 %all-gather = f32[32,1,2,3,3,128]{5,2,4,3,1,0:T(2,128)S(1)} all-gather(f32[1,1,2,3,3,128]{5,2,4,3,1,0:T(2,128)S(1)} %copy.129), channel_id=2, replica_groups=mesh['sec'=4,'mom'=8,'en'=8] {'sec','mom'}, dimensions={0}, use_global_device_ids=true | all-gather | bytes 304128 | tf_op jit(solution)/shard_map/all_gather | solution.py:95
  100.4 232.6 %while.19 = (s32[]{:T(128)}, f32[1,2,2,128,128]{4,3,2,1,0:T(8,128)}, f32[8,4,3,128]{3,2,1,0:T(4,128)}, s32[1,8]{1,0:T(1,128)}, f32[8,4,2,3,3,128]{5,4,3,2,1,0:T(...) while((s32[]{:T(128)}, ...), condition=%wide.region_9.10_spmd.clone, body=%wide.region_8.9_spmd.clone.sunk | while | flops 167619600 | bytes 31974176 | solution.py:128
  100.4 1.3 constant_dynamic-slice_fusion.3
  101.7 1.1 bitcast_convert_fusion.5
  102.9 1.0 fusion.161
  105.3 1.3 convolution_convert_fusion.2
  122.5 6.8 fusion.167
  129.3 1.3 constant_dynamic-slice_fusion.3
  130.6 1.1 bitcast_convert_fusion.5
  131.7 1.0 fusion.161
  134.1 1.3 convolution_convert_fusion.2
  151.3 7.1 fusion.167
  158.4 1.3 constant_dynamic-slice_fusion.3
  159.7 1.1 bitcast_convert_fusion.5
  160.8 1.0 fusion.161
  163.2 1.3 convolution_convert_fusion.2
  180.4 7.1 fusion.167
  187.5 1.3 constant_dynamic-slice_fusion.3
  188.8 1.1 bitcast_convert_fusion.5
  189.9 1.0 fusion.161
  192.3 1.3 convolution_convert_fusion.2
  209.5 7.1 fusion.167
  216.6 1.3 constant_dynamic-slice_fusion.3
  217.9 1.1 bitcast_convert_fusion.5
  219.0 1.0 fusion.161
  221.4 1.3 convolution_convert_fusion.2
  238.7 7.1 fusion.167
  245.7 1.3 constant_dynamic-slice_fusion.3
  247.0 1.1 bitcast_convert_fusion.5
  248.2 1.0 fusion.161
  250.6 1.3 convolution_convert_fusion.2
  267.8 7.1 fusion.167
  274.9 1.3 constant_dynamic-slice_fusion.3
  276.1 1.1 bitcast_convert_fusion.5
  277.3 1.0 fusion.161
  279.7 1.3 convolution_convert_fusion.2
  296.9 7.1 fusion.167
  304.0 1.3 constant_dynamic-slice_fusion.3
  305.3 1.1 bitcast_convert_fusion.5
  308.8 1.3 convolution_convert_fusion.2
  326.0 7.1 fusion.167
  333.1 1.7 broadcast_multiply_fusion
  334.8 728.2 %all-gather.7.cloned.1.call-done = f32[1024,8,3,128]{3,2,0,1:T(4,128)} async-done(((f32[4,8,3,128]{3,2,0,1:T(4,128)}), f32[1024,8,3,128]{3,2,0,1:T(4,128)}) %all-gather.7.cloned.1.call-update) | async-done | bytes 12582928 | tf_op jit(solution)/shard_map/all_gather | solution.py:132
  1062.9 8.8 reduce_sum.89
  (579 shorter events, 140.6 us)
Async XLA Ops:
  7.2 92.7 %copy-start = (s32[8,8]{1,0:T(8,128)S(1)}, s32[8,8]{1,0:T(8,128)}, u32[]{:S(2)}) copy-start(s32[8,8]{1,0:T(8,128)} %param.14) | copy-start | bytes 772
  7.2 92.3 %copy-start.18 = (f32[2]{0:T(128)S(1)}, f32[2]{0:T(128)}, u32[]{:S(2)}) copy-start(f32[2]{0:T(128)} %constant.97.clone) | copy-start | bytes 28
  7.2 92.3 %copy-start.16 = (bf16[1,2,2,128,128]{4,3,2,1,0:T(8,128)(2,1)S(1)}, bf16[1,2,2,128,128]{4,3,2,1,0:T(8,128)(2,1)}, u32[]{:S(2)}) copy-start(bf16[1,2,2,128,128]{4,3,2,1,0:T(8,128)(2,1)} %param.9) | copy-start | bytes 393220
  7.2 92.3 %copy-start.1 = (bf16[3,128,128]{2,1,0:T(8,128)(2,1)S(1)}, bf16[3,128,128]{2,1,0:T(8,128)(2,1)}, u32[]{:S(2)}) copy-start(bf16[3,128,128]{2,1,0:T(8,128)(2,1)} %param.10) | copy-start | bytes 294916
  7.2 93.2 %all-gather.5.cloned.1.call-start = ((), (), s32[]{:S(2)}) async-start(), calls=%async_computation | async-start | bytes 2359296 | tf_op jit(solution)/shard_map/all_gather | solution.py:110
  7.3 12.4 %collective-permute-start = (bf16[1,2,2,128,128]{4,3,2,1,0:T(8,128)(2,1)}, bf16[1,2,2,128,128]{4,3,2,1,0:T(8,128)(2,1)S(1)}, u32[]{:S(2)}, u32[]{:S(2)}) collective-permute-start(bf16[1,2,2,128,128]{4,3,2,1,0:T(8,128)(2,1)} %param.9), channel_id=1, source_target_pairs={{0,1},{1,2},{2,3},{3,4},{4,5},{5,6},{6,7},{7,64},{64,65},{65,66},{... | collective-permute-start | bytes 393224 | tf_op jit(solution)/shard_map/ppermute | solution.py:11
  21.3 1041.6 %all-gather.7.cloned.1.call-start = ((), (), s32[]{:S(2)}) async-start(), calls=%async_computation.1 | async-start | bytes 16842752 | tf_op jit(solution)/shard_map/all_gather | solution.py:132
  116.5 5.8 copy-start.2
  116.6 5.8 copy-start.3
  116.6 5.8 copy-start.4
  116.6 5.8 copy-start.5
  116.6 5.8 copy-start.6
  116.6 5.8 copy-start.7
  145.4 5.8 copy-start.2
  145.4 5.8 copy-start.3
  145.4 5.8 copy-start.4
  145.4 5.8 copy-start.5
  145.4 5.8 copy-start.6
  145.4 5.8 copy-start.7
  174.5 5.8 copy-start.2
  174.5 5.8 copy-start.3
  174.5 5.8 copy-start.4
  174.5 5.8 copy-start.5
  174.5 5.8 copy-start.6
  174.6 5.8 copy-start.7
  203.6 5.8 copy-start.2
  203.6 5.8 copy-start.3
  203.6 5.8 copy-start.4
  203.6 5.8 copy-start.5
  203.7 5.8 copy-start.6
  203.7 5.8 copy-start.7
  232.7 5.8 copy-start.2
  232.7 5.8 copy-start.3
  232.8 5.8 copy-start.4
  232.8 5.8 copy-start.5
  232.8 5.8 copy-start.6
  232.8 5.8 copy-start.7
  261.9 5.8 copy-start.2
  261.9 5.8 copy-start.3
  261.9 5.8 copy-start.4
  261.9 5.8 copy-start.5
  261.9 5.8 copy-start.6
  261.9 5.8 copy-start.7
  291.0 5.8 copy-start.2
  291.0 5.8 copy-start.3
  291.0 5.8 copy-start.4
  291.0 5.8 copy-start.5
  291.0 5.8 copy-start.6
  (79 other events, 213.1 us)
Sparse Core Ops, SparseCore 0:
  21.4 60.1 all-gather.4
  333.2 729.6 all-gather.6
